TPU v7x, 256 devices: a whole 4x4x8 slice. The times are simulated.
256 devices in a mesh: segment: 4 (over y), mp: 16 (over z, core), dp: 4 (over x).
Axes of the slice: x: 4, y: 4, z: 8, core: 2. Of those that a mesh axis runs over, the one named last changes fastest.
Arguments:
- text_rows: bfloat16 [4, 512, 1024], P(None, 'dp'), may hold values from -6 to 6
- durations: int32 [4, 4, 128], P(None, 'dp'), may hold values from 1 to 16, 512 in all within a row
- unit_targets: int32 [4, 2048], P(None, 'dp'), may hold values from 0 to 9999
- w_in: bfloat16 [4, 1024, 8192], P('segment', None, 'mp'), may hold values from -0.1875 to 0.1875
- w_out: bfloat16 [4, 8192, 1024], P('segment', 'mp'), may hold values from -0.0625 to 0.0625
- w_unit: bfloat16 [1024, 10240], P(None, ('segment', 'mp')), as said below
Outputs:
- loss: float32 [4], P('dp')
- grad_in: float32 [4, 1024, 8192], P('segment', 'dp', 'mp')
- grad_out: float32 [4, 8192, 1024], P('segment', 'mp', 'dp')
- grad_unit: float32 [1024, 10240], P('dp', ('segment', 'mp'))
Inputs may be any that keep to these rules, and one draw needn't show every extreme that they name: Within each micro-batch and each index of dp the 128 durations sum to exactly 512, and one of them equals 16. `w_unit`: entries of order 3 / sqrt(1024) in most columns, some columns much larger.
All inputs are finite; a program needn't handle non-finite values.
Results may differ from a plain program's by a relative error of at most 0.035.
Values may be sent and summed in bfloat16 or wider, within the bound.
A program may use at most 128 MiB of HBM per device.

v0:
```python
import jax
import jax.numpy as jnp
from jax import lax
from jax.sharding import PartitionSpec as P


def shifted(block, axis, distance):
    devices = range(lax.axis_size(axis))
    route = [(i - distance, i) for i in devices if i - distance in devices]
    return lax.ppermute(block, axis, route)


def broadcast(x, axis, root):
    mine = lax.axis_index(axis) == root
    return lax.psum(jnp.where(mine, x, jnp.zeros_like(x)), axis)


def gelu_parts(pre_vals):
    coeff = 0.7978845608
    inner = coeff * (pre_vals + 0.044715 * pre_vals * pre_vals * pre_vals)
    tanh_val = jnp.tanh(inner)
    value = 0.5 * pre_vals * (1.0 + tanh_val)
    slope = 0.5 * (1.0 + tanh_val) + 0.5 * pre_vals * (1.0 - tanh_val * tanh_val) * coeff * (
        1.0 + 3.0 * 0.044715 * pre_vals * pre_vals
    )
    return (value, slope)


def row_scale(rows_in):
    floats = rows_in.astype(jnp.float32)
    return lax.rsqrt(jnp.mean(floats * floats, axis=-1, keepdims=True) + 1e-06)


def norm_back(rows_in, grads):
    scale = row_scale(rows_in)
    normal = rows_in.astype(jnp.float32) * scale
    return scale * (grads - normal * jnp.mean(grads * normal, axis=-1, keepdims=True))


def section(rows_in, first):
    normed = (rows_in.astype(jnp.float32) * row_scale(rows_in)).astype(jnp.bfloat16)
    pre_vals = jnp.dot(normed, first, preferred_element_type=jnp.float32)
    value, slope = gelu_parts(pre_vals)
    return (normed, value.astype(jnp.bfloat16), slope)


def finish_forward(pieces, summed):
    return (pieces[0].astype(jnp.float32) + summed).astype(jnp.bfloat16)


def finish_backward(pieces, summed):
    return (pieces[0].astype(jnp.float32) + norm_back(pieces[1], summed)).astype(jnp.bfloat16)


def reduce_rows(partial_value, pieces, finisher):
    summed = lax.psum(partial_value, "mp")
    return finisher(pieces, summed)


def on_device(text_rows, durations, unit_targets, w_in, w_out, w_unit):
    micro_count, row_count, width = text_rows.shape
    segments = lax.axis_size("segment")
    segment_at = lax.axis_index("segment")
    first = w_in[0]
    second = w_out[0]
    clocks = micro_count + segments - 1
    stash = jnp.zeros((micro_count, row_count, width), jnp.bfloat16)
    final_rows = jnp.zeros((micro_count, row_count, width), jnp.bfloat16)
    outgoing = jnp.zeros((row_count, width), jnp.bfloat16)
    for clock in range(clocks):
        if clock > 0:
            incoming = shifted(outgoing, "segment", 1)
        else:
            incoming = jnp.zeros((row_count, width), jnp.bfloat16)
        rows_in = jnp.where(segment_at == 0, text_rows[min(clock, micro_count - 1)], incoming)
        batch_at = clock - segment_at
        is_live = (batch_at >= 0) & (batch_at < micro_count)
        slot_at = jnp.clip(batch_at, 0, micro_count - 1)
        stash = jnp.where(
            is_live, lax.dynamic_update_index_in_dim(stash, rows_in, slot_at, 0), stash
        )
        normed, hidden, slope = section(rows_in, first)
        partial_value = jnp.dot(hidden, second, preferred_element_type=jnp.float32)
        outgoing = reduce_rows(partial_value, (rows_in,), finish_forward)
        is_last = is_live & (segment_at == segments - 1)
        final_rows = jnp.where(
            is_last, lax.dynamic_update_index_in_dim(final_rows, outgoing, slot_at, 0), final_rows
        )
    final_rows = broadcast(final_rows, "segment", segments - 1)
    vocab_part = w_unit.shape[1]
    vocab_start = lax.axis_index(("segment", "mp")) * vocab_part
    final_norm = (final_rows.astype(jnp.float32) * row_scale(final_rows)).astype(jnp.bfloat16)
    logits = jnp.einsum("mrd,dv->mrv", final_norm, w_unit, preferred_element_type=jnp.float32)
    lengths = durations[:, 0, :]
    unit_count = unit_targets.shape[1]
    ends = jnp.cumsum(lengths, axis=-1)
    positions = jnp.arange(unit_count, dtype=jnp.int32)
    row_local = jnp.sum((ends[:, None, :] <= positions[None, :, None]).astype(jnp.int32), axis=-1)
    row_onehot = (
        row_local[:, :, None] == jnp.arange(row_count, dtype=jnp.int32)[None, None, :]
    ).astype(jnp.bfloat16)
    vocab_ids = vocab_start + jnp.arange(vocab_part, dtype=jnp.int32)
    target_hits = (unit_targets[:, :, None] == vocab_ids[None, None, :]).astype(jnp.bfloat16)
    counts = jnp.einsum("mur,muv->mrv", row_onehot, target_hits, preferred_element_type=jnp.float32)
    local_peak = jnp.max(logits, axis=-1)
    target_local = jnp.sum(counts * logits, axis=-1)
    peak = lax.pmax(local_peak, ("segment", "mp"))
    total, target_sum = lax.psum(
        (jnp.sum(jnp.exp(logits - peak[..., None]), axis=-1), target_local), ("segment", "mp")
    )
    lse = peak + jnp.log(total)
    denom = float(micro_count * unit_count * lax.axis_size("dp"))
    length_f = lengths.astype(jnp.float32)
    loss_local = jnp.sum(length_f * lse - target_sum)
    loss = (loss_local / denom)[None]
    dlogits = ((length_f[..., None] * jnp.exp(logits - lse[..., None]) - counts) / denom).astype(
        jnp.bfloat16
    )
    grad_unit = jnp.einsum("mrd,mrv->dv", final_norm, dlogits, preferred_element_type=jnp.float32)
    norm_part = jnp.einsum("mrv,dv->mrd", dlogits, w_unit, preferred_element_type=jnp.float32)
    norm_share = lax.psum_scatter(
        norm_part, ("segment", "mp"), scatter_dimension=2, tiled=True
    ).astype(jnp.bfloat16)
    dnorm = lax.all_gather(norm_share, ("segment", "mp"), axis=2, tiled=True)
    grad_final = norm_back(final_rows, dnorm.astype(jnp.float32)).astype(jnp.bfloat16)
    grad_first = jnp.zeros(first.shape, jnp.float32)
    grad_second = jnp.zeros(second.shape, jnp.float32)
    going_back = jnp.zeros((row_count, width), jnp.bfloat16)
    for clock in range(clocks):
        if clock > 0:
            arriving = shifted(going_back, "segment", -1)
        else:
            arriving = jnp.zeros((row_count, width), jnp.bfloat16)
        grad_rows = jnp.where(
            segment_at == segments - 1, grad_final[min(clock, micro_count - 1)], arriving
        )
        batch_at = clock - (segments - 1 - segment_at)
        is_live = (batch_at >= 0) & (batch_at < micro_count)
        slot_at = jnp.clip(batch_at, 0, micro_count - 1)
        rows_in = lax.dynamic_index_in_dim(stash, slot_at, 0, keepdims=False)
        normed, hidden, slope = section(rows_in, first)
        live_f = is_live.astype(jnp.float32)
        grad_second = grad_second + live_f * jnp.dot(
            hidden.T, grad_rows, preferred_element_type=jnp.float32
        )
        dhidden = jnp.dot(grad_rows, second.T, preferred_element_type=jnp.float32)
        dpre = (dhidden * slope).astype(jnp.bfloat16)
        grad_first = grad_first + live_f * jnp.dot(
            normed.T, dpre, preferred_element_type=jnp.float32
        )
        dnormed = jnp.dot(dpre, first.T, preferred_element_type=jnp.float32)
        going_back = reduce_rows(dnormed, (grad_rows, rows_in), finish_backward)
    sum_first, sum_second, sum_unit = (
        lax.psum_scatter(grad_first, "dp", scatter_dimension=0, tiled=True),
        lax.psum_scatter(grad_second, "dp", scatter_dimension=1, tiled=True),
        lax.psum_scatter(grad_unit, "dp", scatter_dimension=0, tiled=True),
    )
    return (loss, sum_first[None], sum_second[None], sum_unit)


def solution(mesh):
    placed = (
        P(None, "dp", None),
        P(None, "dp", None),
        P(None, "dp"),
        P("segment", None, "mp"),
        P("segment", "mp", None),
        P(None, ("segment", "mp")),
    )
    return jax.shard_map(
        on_device,
        mesh=mesh,
        in_specs=placed,
        out_specs=(
            P("dp"),
            P("segment", "dp", "mp"),
            P("segment", "mp", "dp"),
            P("dp", ("segment", "mp")),
        ),
        check_vma=False,
    )
```

profile of v0, /device:TPU:1, one launch (start us, length us, event | category | flops | bytes accessed | tf_op | source)
XLA Modules:
  0.0 2379.7 jit_solution(6565013018614124377)
XLA Ops:
  8.5 2.7 fusion.35
  11.3 113.5 %all-reduce.18.cloned.1.call-done = f32[128,1024]{1,0:T(8,128)} async-done(((f32[128,1024]{1,0:T(8,128)}), f32[128,1024]{1,0:T(8,128)}) %all-reduce.18.cloned.1.call-update) | async-done | bytes 524304 | tf_op jit(solution)/shard_map/psum | solution.py:56
  126.2 3.8 collective-permute-start
  131.2 3.0 collective-permute-done
  137.0 111.0 %all-reduce.20.cloned.1.call-done = f32[128,1024]{1,0:T(8,128)} async-done(((f32[128,1024]{1,0:T(8,128)}), f32[128,1024]{1,0:T(8,128)}) %all-reduce.20.cloned.1.call-update) | async-done | bytes 524304 | tf_op jit(solution)/shard_map/psum | solution.py:56
  248.0 2.0 fusion.308
  250.1 3.1 collective-permute-start.1
  253.2 5.2 collective-permute-done.1
  261.9 110.8 %all-reduce.22.cloned.1.call-done = f32[128,1024]{1,0:T(8,128)} async-done(((f32[128,1024]{1,0:T(8,128)}), f32[128,1024]{1,0:T(8,128)}) %all-reduce.22.cloned.1.call-update) | async-done | bytes 524304 | tf_op jit(solution)/shard_map/psum | solution.py:56
  372.6 2.0 fusion.307
  374.7 3.1 collective-permute-start.2
  377.8 5.2 collective-permute-done.2
  386.5 110.8 %all-reduce.24.cloned.1.call-done = f32[128,1024]{1,0:T(8,128)} async-done(((f32[128,1024]{1,0:T(8,128)}), f32[128,1024]{1,0:T(8,128)}) %all-reduce.24.cloned.1.call-update) | async-done | bytes 524304 | tf_op jit(solution)/shard_map/psum | solution.py:56
  497.3 2.0 fusion.306
  499.3 3.1 collective-permute-start.3
  502.4 5.2 collective-permute-done.3
  511.1 110.8 %all-reduce.26.cloned.1.call-done = f32[128,1024]{1,0:T(8,128)} async-done(((f32[128,1024]{1,0:T(8,128)}), f32[128,1024]{1,0:T(8,128)}) %all-reduce.26.cloned.1.call-update) | async-done | bytes 524304 | tf_op jit(solution)/shard_map/psum | solution.py:56
  621.9 2.0 fusion.305
  623.9 3.1 collective-permute-start.4
  627.0 5.2 collective-permute-done.4
  635.7 110.8 %all-reduce.28.cloned.1.call-done = f32[128,1024]{1,0:T(8,128)} async-done(((f32[128,1024]{1,0:T(8,128)}), f32[128,1024]{1,0:T(8,128)}) %all-reduce.28.cloned.1.call-update) | async-done | bytes 524304 | tf_op jit(solution)/shard_map/psum | solution.py:56
  746.5 2.0 fusion.304
  748.5 3.1 collective-permute-start.5
  751.7 5.2 collective-permute-done.5
  760.3 110.8 %all-reduce.30.cloned.1.call-done = f32[128,1024]{1,0:T(8,128)} async-done(((f32[128,1024]{1,0:T(8,128)}), f32[128,1024]{1,0:T(8,128)}) %all-reduce.30.cloned.1.call-update) | async-done | bytes 524304 | tf_op jit(solution)/shard_map/psum | solution.py:56
  871.1 2.0 fusion.259
  876.2 49.1 %all-reduce.32.cloned.1.call-done = bf16[4,128,1024]{2,1,0:T(8,128)(2,1)} async-done(((bf16[4,128,1024]{2,1,0:T(8,128)(2,1)}), bf16[4,128,1024]{2,1,0:T(8,128)(2,1)}) %all-reduce.32.cloned.1.call-update) | async-done | bytes 1048592 | tf_op jit(solution)/shard_map/psum | solution.py:15
  926.8 2.5 fusion.571
  929.3 125.5 %pmax.7 = f32[4,128]{1,0:T(4,128)S(1)} all-reduce(f32[4,128]{1,0:T(4,128)S(1)} %get-tuple-element.40), channel_id=1, replica_groups=mesh['segment'=4,'mp'=16,'dp'=4] {'segment','mp'}, use_global_device_ids=true, to_apply=%region_17.18 | all-reduce | flops 512 | bytes 4096 | tf_op jit(solution)/shard_map/pmax | solution.py:107
  1054.8 2.3 exponential_reduce_fusion
  1057.1 127.1 %psum.120 = f32[4,128]{1,0:T(4,128)S(1)} all-reduce(f32[4,128]{1,0:T(4,128)S(1)} %get-tuple-element.12), channel_id=1, replica_groups=mesh['segment'=4,'mp'=16,'dp'=4] {'segment','mp'}, use_global_device_ids=true, to_apply=%region_19.20 | all-reduce | flops 512 | bytes 4096 | tf_op jit(solution)/shard_map/psum | solution.py:108
  1186.5 2.7 copy.13
  1189.2 265.5 %all-reduce.45 = (f32[4,128]{1,0:T(4,128)}, bf16[4,128,1024]{1,0,2:T(4,128)(2,1)}) all-reduce(f32[4,128]{1,0:T(4,128)S(1)} %get-tuple-element.13, f32[4,128,1024]{1,0,2:T(4,128)} %copy.13), channel_id=1, replica_groups=mesh['segment'=4,'mp'=16,'dp'=4] {'segment','mp'}, use_global_device_ids=true, to_apply=%region_23.24 | all-reduce | flops 524800 | bytes 3149824 | tf_op jit(solution)/shard_map/psum | solution.py:108
  1456.9 75.1 %all-gather.2.cloned.1.call-done = bf16[4,128,1024]{1,0,2:T(4,128)(2,1)} async-done(((bf16[4,128,16]{1,0,2:T(4,128)(2,1)}), bf16[4,128,1024]{1,0,2:T(4,128)(2,1)}) %all-gather.2.cloned.1.call-update) | async-done | bytes 1048592 | tf_op jit(solution)/shard_map/all_gather | solution.py:124
  1531.9 2.5 copy.14
  1534.4 2.2 fusion.3
  1540.1 106.9 %all-reduce.34.cloned.1.call-done = f32[128,1024]{1,0:T(8,128)} async-done(((f32[128,1024]{1,0:T(8,128)}), f32[128,1024]{1,0:T(8,128)}) %all-reduce.34.cloned.1.call-update) | async-done | bytes 524304 | tf_op jit(solution)/shard_map/psum | solution.py:56
  1647.0 2.2 fusion.159
  1651.1 7.3 collective-permute-done.6
  1661.0 109.8 %all-reduce.36.cloned.1.call-done = f32[128,1024]{1,0:T(8,128)} async-done(((f32[128,1024]{1,0:T(8,128)}), f32[128,1024]{1,0:T(8,128)}) %all-reduce.36.cloned.1.call-update) | async-done | bytes 524304 | tf_op jit(solution)/shard_map/psum | solution.py:56
  1775.8 6.7 collective-permute-done.7
  1786.7 109.8 %all-reduce.38.cloned.1.call-done = f32[128,1024]{1,0:T(8,128)} async-done(((f32[128,1024]{1,0:T(8,128)}), f32[128,1024]{1,0:T(8,128)}) %all-reduce.38.cloned.1.call-update) | async-done | bytes 524304 | tf_op jit(solution)/shard_map/psum | solution.py:56
  1901.5 6.7 collective-permute-done.8
  1912.4 109.8 %all-reduce.40.cloned.1.call-done = f32[128,1024]{1,0:T(8,128)} async-done(((f32[128,1024]{1,0:T(8,128)}), f32[128,1024]{1,0:T(8,128)}) %all-reduce.40.cloned.1.call-update) | async-done | bytes 524304 | tf_op jit(solution)/shard_map/psum | solution.py:56
  2027.3 6.7 collective-permute-done.9
  2038.2 109.8 %all-reduce.42.cloned.1.call-done = f32[128,1024]{1,0:T(8,128)} async-done(((f32[128,1024]{1,0:T(8,128)}), f32[128,1024]{1,0:T(8,128)}) %all-reduce.42.cloned.1.call-update) | async-done | bytes 524304 | tf_op jit(solution)/shard_map/psum | solution.py:56
  2153.0 6.7 collective-permute-done.10
  2164.0 2.6 convolution_bitcast_fusion
  2166.9 2.9 fusion.403
  2169.9 1.8 fusion.418
  2173.5 1.8 fusion.420
  2175.3 1.9 fusion.421
  2178.9 94.8 %all-reduce.44.cloned.1.call-done = f32[128,1024]{1,0:T(8,128)} async-done(((f32[128,1024]{1,0:T(8,128)}), f32[128,1024]{1,0:T(8,128)}) %all-reduce.44.cloned.1.call-update) | async-done | bytes 524304 | tf_op jit(solution)/shard_map/psum | solution.py:56
  2278.2 7.3 collective-permute-done.11
  2286.2 6.7 multiply_add_fusion
  2293.0 2.6 fusion.283
  2295.6 1.8 fusion.285
  2297.5 1.9 fusion.287
  2299.3 1.9 fusion.289
  2301.2 1.9 fusion.291
  2303.1 1.9 fusion.293
  2305.0 7.7 multiply_add_fusion.1
  2314.6 21.9 reduce-scatter.6.cloned.1.call-done
  2336.6 35.2 %reduce-scatter.4.cloned.1.call-done = f32[256,512]{1,0:T(8,128)} async-done(((f32[1024,512]{1,0:T(8,128)}), f32[256,512]{1,0:T(8,128)}) %reduce-scatter.4.cloned.1.call-update) | async-done | bytes 524304 | tf_op jit(solution)/shard_map/reduce_scatter | solution.py:154
  (261 shorter events, 86.9 us)
Async XLA Ops:
  7.2 117.6 %all-reduce.18.cloned.1.call-start = ((), (), s32[]{:S(2)}) async-start(), calls=%async_computation.3 | async-start | bytes 1048576 | tf_op jit(solution)/shard_map/psum | solution.py:56
  11.2 236.8 %all-reduce.20.cloned.1.call-start = ((), (), s32[]{:S(2)}) async-start(), calls=%async_computation.4 | async-start | bytes 1048576 | tf_op jit(solution)/shard_map/psum | solution.py:56
  124.9 10.6 copy-start.1
  126.2 3.8 copy-start.3
  126.2 8.0 collective-permute-start
  137.0 235.7 %all-reduce.22.cloned.1.call-start = ((), (), s32[]{:S(2)}) async-start(), calls=%async_computation.5 | async-start | bytes 1048576 | tf_op jit(solution)/shard_map/psum | solution.py:56
  250.1 8.3 collective-permute-start.1
  261.8 235.4 %all-reduce.24.cloned.1.call-start = ((), (), s32[]{:S(2)}) async-start(), calls=%async_computation.6 | async-start | bytes 1048576 | tf_op jit(solution)/shard_map/psum | solution.py:56
  374.7 8.3 collective-permute-start.2
  386.4 235.4 %all-reduce.26.cloned.1.call-start = ((), (), s32[]{:S(2)}) async-start(), calls=%async_computation.7 | async-start | bytes 1048576 | tf_op jit(solution)/shard_map/psum | solution.py:56
  499.3 8.3 collective-permute-start.3
  511.0 235.4 %all-reduce.28.cloned.1.call-start = ((), (), s32[]{:S(2)}) async-start(), calls=%async_computation.8 | async-start | bytes 1048576 | tf_op jit(solution)/shard_map/psum | solution.py:56
  623.9 8.3 collective-permute-start.4
  635.7 235.4 %all-reduce.30.cloned.1.call-start = ((), (), s32[]{:S(2)}) async-start(), calls=%async_computation.9 | async-start | bytes 1048576 | tf_op jit(solution)/shard_map/psum | solution.py:56
  748.5 8.3 collective-permute-start.5
  760.3 165.0 %all-reduce.32.cloned.1.call-start = ((), (), s32[]{:S(2)}) async-start(), calls=%async_computation.10 | async-start | bytes 2097152 | tf_op jit(solution)/shard_map/psum | solution.py:15
  871.1 3.5 copy-start.60
  873.1 53.7 %copy-start.40 = (bf16[1024,160]{0,1:T(8,128)(2,1)S(1)}, bf16[1024,160]{0,1:T(8,128)(2,1)}, u32[]{:S(2)}) copy-start(bf16[1024,160]{0,1:T(8,128)(2,1)} %param.11) | copy-start | bytes 983044
  874.2 180.6 %copy-start.59 = (s32[4,512]{1,0:T(4,128)S(1)}, s32[4,512]{1,0:T(4,128)}, u32[]{:S(2)}) copy-start(s32[4,512]{1,0:T(4,128)} %param.8) | copy-start | bytes 24580
  874.2 657.7 %all-gather.2.cloned.1.call-start = ((), (), s32[]{:S(2)}) async-start(), calls=%async_computation.11 | async-start | bytes 1064960 | tf_op jit(solution)/shard_map/all_gather | solution.py:124
  1456.1 190.9 %all-reduce.34.cloned.1.call-start = ((), (), s32[]{:S(2)}) async-start(), calls=%async_computation.12 | async-start | bytes 1048576 | tf_op jit(solution)/shard_map/psum | solution.py:56
  1456.5 192.7 %copy-start.55 = (f32[128]{0:T(128)}, f32[128]{0:T(128)S(1)}, u32[]{:S(2)}) copy-start(f32[128]{0:T(128)S(1)} %add_rsqrt_fusion.7) | copy-start | bytes 1540
  1456.9 80.3 %copy-start.29 = (f32[128,512]{1,0:T(8,128)}, f32[128,512]{1,0:T(8,128)S(1)}, u32[]{:S(2)}) copy-start(f32[128,512]{1,0:T(8,128)S(1)} %fusion.61) | copy-start | bytes 786436
  1540.0 230.8 %all-reduce.36.cloned.1.call-start = ((), (), s32[]{:S(2)}) async-start(), calls=%async_computation.13 | async-start | bytes 1048576 | tf_op jit(solution)/shard_map/psum | solution.py:56
  1649.4 9.0 collective-permute-start.6
  1650.7 121.4 %copy-start.47 = (f32[128]{0:T(128)}, f32[128]{0:T(128)S(1)}, u32[]{:S(2)}) copy-start(f32[128]{0:T(128)S(1)} %add_rsqrt_fusion.6) | copy-start | bytes 1540
  1651.1 7.4 copy-start.19
  1661.0 235.5 %all-reduce.38.cloned.1.call-start = ((), (), s32[]{:S(2)}) async-start(), calls=%async_computation.14 | async-start | bytes 1048576 | tf_op jit(solution)/shard_map/psum | solution.py:56
  1773.4 9.0 collective-permute-start.7
  1775.4 122.4 %copy-start.49 = (f32[128]{0:T(128)}, f32[128]{0:T(128)S(1)}, u32[]{:S(2)}) copy-start(f32[128]{0:T(128)S(1)} %add_rsqrt_fusion.5) | copy-start | bytes 1540
  1775.7 8.9 copy-start.21
  1786.6 235.6 %all-reduce.40.cloned.1.call-start = ((), (), s32[]{:S(2)}) async-start(), calls=%async_computation.15 | async-start | bytes 1048576 | tf_op jit(solution)/shard_map/psum | solution.py:56
  1899.1 9.0 collective-permute-start.8
  1901.1 122.4 %copy-start.51 = (f32[128]{0:T(128)}, f32[128]{0:T(128)S(1)}, u32[]{:S(2)}) copy-start(f32[128]{0:T(128)S(1)} %add_rsqrt_fusion.4) | copy-start | bytes 1540
  1901.5 8.9 copy-start.23
  1912.4 235.6 %all-reduce.42.cloned.1.call-start = ((), (), s32[]{:S(2)}) async-start(), calls=%async_computation.16 | async-start | bytes 1048576 | tf_op jit(solution)/shard_map/psum | solution.py:56
  2024.9 9.0 collective-permute-start.9
  2026.9 122.4 %copy-start.53 = (f32[128]{0:T(128)}, f32[128]{0:T(128)S(1)}, u32[]{:S(2)}) copy-start(f32[128]{0:T(128)S(1)} %add_rsqrt_fusion.3) | copy-start | bytes 1540
  2027.2 8.9 copy-start.25
  2038.1 235.6 %all-reduce.44.cloned.1.call-start = ((), (), s32[]{:S(2)}) async-start(), calls=%async_computation.17 | async-start | bytes 1048576 | tf_op jit(solution)/shard_map/psum | solution.py:56
  2150.7 9.0 collective-permute-start.10
  2153.0 9.0 copy-start.27
  2163.9 150.7 %reduce-scatter.8.cloned.1.call-start = ((), (), s32[]{:S(2)}) async-start(), calls=%async_computation.20 | async-start | bytes 819200 | tf_op jit(solution)/shard_map/reduce_scatter | solution.py:156
  2166.6 169.9 %reduce-scatter.6.cloned.1.call-start = ((), (), s32[]{:S(2)}) async-start(), calls=%async_computation.19 | async-start | bytes 2621440 | tf_op jit(solution)/shard_map/reduce_scatter | solution.py:155
  2166.9 4.8 copy-start.9
  2166.9 4.8 copy-start.22
  2169.9 3.6 copy-start.11
  2169.9 3.6 copy-start.24
  2171.7 3.6 copy-start.13
  2171.7 3.6 copy-start.26
  2173.5 3.7 copy-start.15
  2173.5 3.7 copy-start.28
  2273.8 12.4 copy-start.7
  2276.5 9.0 collective-permute-start.11
  2277.8 15.1 copy-start.56
  2292.9 78.8 %reduce-scatter.4.cloned.1.call-start = ((), (), s32[]{:S(2)}) async-start(), calls=%async_computation.18 | async-start | bytes 2621440 | tf_op jit(solution)/shard_map/reduce_scatter | solution.py:154
  2293.0 4.5 copy-start.33
  2293.0 4.5 copy-start.50
  2295.6 3.7 copy-start.35
  2295.6 3.7 copy-start.52
  2297.5 3.8 copy-start.37
  2297.5 3.8 copy-start.54
  2299.3 3.8 copy-start.39
  2301.2 3.8 copy-start.57
  (27 other events, 34.2 us)
Sparse Core Ops, SparseCore 0:
  11.4 113.3 all-reduce.17
  137.1 110.8 all-reduce.19
  261.9 110.6 all-reduce.21
  386.5 110.6 all-reduce.23
  511.2 110.6 all-reduce.25
  635.8 110.6 all-reduce.27
  760.4 110.6 all-reduce.29
  874.3 50.9 all-reduce.31
  1456.2 75.6 all-gather.1
  1540.1 106.8 all-reduce.33
  1661.1 109.7 all-reduce.35
  1786.8 109.7 all-reduce.37
  1912.5 109.7 all-reduce.39
  2038.3 109.7 all-reduce.41
  2164.0 109.6 all-reduce.43
  2276.7 23.4 reduce-scatter.7
  2303.2 33.2 reduce-scatter.5
  2339.7 31.9 reduce-scatter.3
where the time goes:
time: 2380 us
  waiting for transfers between devices  1670 us (70%)
  blocking collectives  518 us (22%)
  matrix products  70.9 us (3%)
  other arithmetic  53.3 us (2%)
  starting transfers between devices  28.3 us (1%)
    psum x13, waiting for transfers between devices, reduce_rows(): summed = lax.psum(partial_value, 'mp')  1420 us
    psum x2, blocking collectives, on_device(): lax.psum((jnp.sum(jnp.exp(logits - peak[..., None]), axis=-1), target_loc...  393 us
    pmax x1, blocking collectives, on_device(): peak = lax.pmax(local_peak, ('segment', 'mp'))  125 us
    all_gather x1, waiting for transfers between devices, on_device(): dnorm = lax.all_gather(norm_share, ('segment', 'mp'), axis=2, tiled=True)  75.1 us
    ppermute x12, waiting for transfers between devices, shifted(): return lax.ppermute(block, axis, route)  70.4 us
    psum x1, waiting for transfers between devices, broadcast(): return lax.psum(jnp.where(mine, x, jnp.zeros_like(x)), axis)  49.1 us
  transfers between devices with their start and end apart: 30, of which 29 were waited for; matrix products, arithmetic and copies ran while one was open for 2% of the time, Pallas kernels for 0%

commit v1 on v0

--- a/solution.py
+++ b/solution.py
@@ -106,7 +106,8 @@
     target_local = jnp.sum(counts * logits, axis=-1)
     peak = lax.pmax(local_peak, ("segment", "mp"))
     total, target_sum = lax.psum(
-        (jnp.sum(jnp.exp(logits - peak[..., None]), axis=-1), target_local), ("segment", "mp")
+        lax.psum((jnp.sum(jnp.exp(logits - peak[..., None]), axis=-1), target_local), "mp"),
+        "segment",
     )
     lse = peak + jnp.log(total)
     denom = float(micro_count * unit_count * lax.axis_size("dp"))

time: 2380 us -> 2290 us (0.962)
  blocking collectives: 518 us -> 422 us
    psum x2 -> x1, blocking collectives: 393 us -> 26.6 us  [on_device(): lax.psum((jnp.sum(jnp.exp(logits - peak[..., None]), axis=-1), target_loc...]
    unnamed x0 -> x1, blocking collectives: none -> 264 us
where the time goes in v1:
time: 2290 us; the launch traced here: 2280 us
  waiting for transfers between devices  1670 us (73%)
  blocking collectives  422 us (18%)
  matrix products  70.2 us (3%)
  other arithmetic  53.2 us (2%)
  starting transfers between devices  28.3 us (1%)
    psum x13, waiting for transfers between devices, reduce_rows(): summed = lax.psum(partial_value, 'mp')  1420 us
    unnamed x1, blocking collectives  264 us
    pmax x1, blocking collectives, on_device(): peak = lax.pmax(local_peak, ('segment', 'mp'))  125 us
    all_gather x1, waiting for transfers between devices, on_device(): dnorm = lax.all_gather(norm_share, ('segment', 'mp'), axis=2, tiled=True)  75 us
    ppermute x12, waiting for transfers between devices, shifted(): return lax.ppermute(block, axis, route)  70.6 us
    psum x1, waiting for transfers between devices, broadcast(): return lax.psum(jnp.where(mine, x, jnp.zeros_like(x)), axis)  49.1 us
  transfers between devices with their start and end apart: 30, of which 29 were waited for; matrix products, arithmetic and copies ran while one was open for 2% of the time, Pallas kernels for 0%

profile of v1, /device:TPU:1, one launch (start us, length us, event | category | flops | bytes accessed | tf_op | source)
XLA Modules:
  0.0 2284.3 jit_solution(13711070118040740158)
XLA Ops:
  8.5 2.7 fusion.35
  11.3 113.5 %all-reduce.19.cloned.1.call-done = f32[128,1024]{1,0:T(8,128)} async-done(((f32[128,1024]{1,0:T(8,128)}), f32[128,1024]{1,0:T(8,128)}) %all-reduce.19.cloned.1.call-update) | async-done | bytes 524304 | tf_op jit(solution)/shard_map/psum | solution.py:56
  126.2 3.8 collective-permute-start
  131.2 3.0 collective-permute-done
  137.0 111.0 %all-reduce.21.cloned.1.call-done = f32[128,1024]{1,0:T(8,128)} async-done(((f32[128,1024]{1,0:T(8,128)}), f32[128,1024]{1,0:T(8,128)}) %all-reduce.21.cloned.1.call-update) | async-done | bytes 524304 | tf_op jit(solution)/shard_map/psum | solution.py:56
  248.0 2.0 fusion.308
  250.1 3.1 collective-permute-start.1
  253.2 5.2 collective-permute-done.1
  261.9 110.8 %all-reduce.23.cloned.1.call-done = f32[128,1024]{1,0:T(8,128)} async-done(((f32[128,1024]{1,0:T(8,128)}), f32[128,1024]{1,0:T(8,128)}) %all-reduce.23.cloned.1.call-update) | async-done | bytes 524304 | tf_op jit(solution)/shard_map/psum | solution.py:56
  372.7 2.0 fusion.307
  374.7 3.1 collective-permute-start.2
  377.8 5.2 collective-permute-done.2
  386.5 110.8 %all-reduce.25.cloned.1.call-done = f32[128,1024]{1,0:T(8,128)} async-done(((f32[128,1024]{1,0:T(8,128)}), f32[128,1024]{1,0:T(8,128)}) %all-reduce.25.cloned.1.call-update) | async-done | bytes 524304 | tf_op jit(solution)/shard_map/psum | solution.py:56
  497.3 2.1 fusion.306
  499.3 3.1 collective-permute-start.3
  502.4 5.2 collective-permute-done.3
  511.1 110.8 %all-reduce.27.cloned.1.call-done = f32[128,1024]{1,0:T(8,128)} async-done(((f32[128,1024]{1,0:T(8,128)}), f32[128,1024]{1,0:T(8,128)}) %all-reduce.27.cloned.1.call-update) | async-done | bytes 524304 | tf_op jit(solution)/shard_map/psum | solution.py:56
  621.9 2.1 fusion.305
  623.9 3.1 collective-permute-start.4
  627.1 5.2 collective-permute-done.4
  635.7 110.8 %all-reduce.29.cloned.1.call-done = f32[128,1024]{1,0:T(8,128)} async-done(((f32[128,1024]{1,0:T(8,128)}), f32[128,1024]{1,0:T(8,128)}) %all-reduce.29.cloned.1.call-update) | async-done | bytes 524304 | tf_op jit(solution)/shard_map/psum | solution.py:56
  746.5 2.1 fusion.304
  748.6 3.1 collective-permute-start.5
  751.7 5.2 collective-permute-done.5
  760.4 110.8 %all-reduce.31.cloned.1.call-done = f32[128,1024]{1,0:T(8,128)} async-done(((f32[128,1024]{1,0:T(8,128)}), f32[128,1024]{1,0:T(8,128)}) %all-reduce.31.cloned.1.call-update) | async-done | bytes 524304 | tf_op jit(solution)/shard_map/psum | solution.py:56
  871.1 2.0 fusion.259
  876.2 49.1 %all-reduce.33.cloned.1.call-done = bf16[4,128,1024]{2,1,0:T(8,128)(2,1)} async-done(((bf16[4,128,1024]{2,1,0:T(8,128)(2,1)}), bf16[4,128,1024]{2,1,0:T(8,128)(2,1)}) %all-reduce.33.cloned.1.call-update) | async-done | bytes 1048592 | tf_op jit(solution)/shard_map/psum | solution.py:15
  926.8 2.5 fusion.571
  929.4 125.5 %pmax.7 = f32[4,128]{1,0:T(4,128)S(1)} all-reduce(f32[4,128]{1,0:T(4,128)S(1)} %get-tuple-element.44), channel_id=1, replica_groups=mesh['segment'=4,'mp'=16,'dp'=4] {'segment','mp'}, use_global_device_ids=true, to_apply=%region_17.18 | all-reduce | flops 512 | bytes 4096 | tf_op jit(solution)/shard_map/pmax | solution.py:107
  1054.8 2.3 exponential_reduce_fusion
  1057.1 26.6 %all-reduce.1 = (f32[4,128]{1,0:T(4,128)S(1)}, f32[4,128]{1,0:T(4,128)S(1)}) all-reduce(f32[4,128]{1,0:T(4,128)S(1)} %get-tuple-element.13, f32[4,128]{1,0:T(4,128)S(1)} %get-tuple-element.12), channel_id=1, replica_groups=mesh['segment'=4,'mp'=16,'dp'=4] {'mp'}, use_global_device_ids=true, to_apply=%region_24.25 | all-reduce | flops 1024 | bytes 8192 | tf_op jit(solution)/shard_map/psum | solution.py:109
  1083.7 6.0 all-reduce.2
  1092.6 2.7 copy.13
  1095.4 264.3 %all-reduce.46 = bf16[4,128,1024]{1,0,2:T(4,128)(2,1)} all-reduce(f32[4,128,1024]{1,0,2:T(4,128)} %copy.13), channel_id=2, replica_groups=mesh['segment'=4,'mp'=16,'dp'=4] {'segment','mp'}, use_global_device_ids=true, to_apply=%region_28.29.clone | all-reduce | flops 524288 | bytes 3145728
  1361.8 75.0 %all-gather.2.cloned.1.call-done = bf16[4,128,1024]{1,0,2:T(4,128)(2,1)} async-done(((bf16[4,128,16]{1,0,2:T(4,128)(2,1)}), bf16[4,128,1024]{1,0,2:T(4,128)(2,1)}) %all-gather.2.cloned.1.call-update) | async-done | bytes 1048592 | tf_op jit(solution)/shard_map/all_gather | solution.py:125
  1436.8 2.5 copy.14
  1439.3 2.2 fusion.3
  1444.9 106.9 %all-reduce.35.cloned.1.call-done = f32[128,1024]{1,0:T(8,128)} async-done(((f32[128,1024]{1,0:T(8,128)}), f32[128,1024]{1,0:T(8,128)}) %all-reduce.35.cloned.1.call-update) | async-done | bytes 524304 | tf_op jit(solution)/shard_map/psum | solution.py:56
  1551.9 2.1 fusion.159
  1555.9 7.3 collective-permute-done.6
  1565.9 109.8 %all-reduce.37.cloned.1.call-done = f32[128,1024]{1,0:T(8,128)} async-done(((f32[128,1024]{1,0:T(8,128)}), f32[128,1024]{1,0:T(8,128)}) %all-reduce.37.cloned.1.call-update) | async-done | bytes 524304 | tf_op jit(solution)/shard_map/psum | solution.py:56
  1680.6 6.7 collective-permute-done.7
  1691.5 109.6 %all-reduce.39.cloned.1.call-done = f32[128,1024]{1,0:T(8,128)} async-done(((f32[128,1024]{1,0:T(8,128)}), f32[128,1024]{1,0:T(8,128)}) %all-reduce.39.cloned.1.call-update) | async-done | bytes 524304 | tf_op jit(solution)/shard_map/psum | solution.py:56
  1806.1 6.7 collective-permute-done.8
  1817.0 109.8 %all-reduce.41.cloned.1.call-done = f32[128,1024]{1,0:T(8,128)} async-done(((f32[128,1024]{1,0:T(8,128)}), f32[128,1024]{1,0:T(8,128)}) %all-reduce.41.cloned.1.call-update) | async-done | bytes 524304 | tf_op jit(solution)/shard_map/psum | solution.py:56
  1931.7 6.8 collective-permute-done.9
  1942.8 109.8 %all-reduce.43.cloned.1.call-done = f32[128,1024]{1,0:T(8,128)} async-done(((f32[128,1024]{1,0:T(8,128)}), f32[128,1024]{1,0:T(8,128)}) %all-reduce.43.cloned.1.call-update) | async-done | bytes 524304 | tf_op jit(solution)/shard_map/psum | solution.py:56
  2057.6 6.7 collective-permute-done.10
  2068.6 2.6 convolution_bitcast_fusion
  2071.5 2.9 fusion.403
  2074.4 1.8 fusion.418
  2079.8 1.9 fusion.421
  2083.5 94.8 %all-reduce.45.cloned.1.call-done = f32[128,1024]{1,0:T(8,128)} async-done(((f32[128,1024]{1,0:T(8,128)}), f32[128,1024]{1,0:T(8,128)}) %all-reduce.45.cloned.1.call-update) | async-done | bytes 524304 | tf_op jit(solution)/shard_map/psum | solution.py:56
  2182.7 7.3 collective-permute-done.11
  2190.8 6.7 multiply_add_fusion
  2198.1 1.9 fusion.283
  2200.0 1.8 fusion.285
  2201.8 1.9 fusion.287
  2203.7 1.9 fusion.289
  2205.6 1.9 fusion.291
  2207.5 1.9 fusion.293
  2209.4 7.7 multiply_add_fusion.1
  2217.8 23.4 %reduce-scatter.6.cloned.1.call-done = f32[512,256]{1,0:T(8,128)} async-done(((f32[512,1024]{1,0:T(8,128)}), f32[512,256]{1,0:T(8,128)}) %reduce-scatter.6.cloned.1.call-update) | async-done | bytes 524304 | tf_op jit(solution)/shard_map/reduce_scatter | solution.py:156
  2241.1 35.2 %reduce-scatter.4.cloned.1.call-done = f32[256,512]{1,0:T(8,128)} async-done(((f32[1024,512]{1,0:T(8,128)}), f32[256,512]{1,0:T(8,128)}) %reduce-scatter.4.cloned.1.call-update) | async-done | bytes 524304 | tf_op jit(solution)/shard_map/reduce_scatter | solution.py:155
  (253 shorter events, 88.3 us)
Async XLA Ops:
  7.2 117.6 %all-reduce.19.cloned.1.call-start = ((), (), s32[]{:S(2)}) async-start(), calls=%async_computation.3 | async-start | bytes 1048576 | tf_op jit(solution)/shard_map/psum | solution.py:56
  11.2 236.8 %all-reduce.21.cloned.1.call-start = ((), (), s32[]{:S(2)}) async-start(), calls=%async_computation.4 | async-start | bytes 1048576 | tf_op jit(solution)/shard_map/psum | solution.py:56
  124.9 10.6 copy-start.1
  126.2 3.9 copy-start.3
  126.2 8.0 collective-permute-start
  137.0 235.7 %all-reduce.23.cloned.1.call-start = ((), (), s32[]{:S(2)}) async-start(), calls=%async_computation.5 | async-start | bytes 1048576 | tf_op jit(solution)/shard_map/psum | solution.py:56
  250.1 8.3 collective-permute-start.1
  261.8 235.4 %all-reduce.25.cloned.1.call-start = ((), (), s32[]{:S(2)}) async-start(), calls=%async_computation.6 | async-start | bytes 1048576 | tf_op jit(solution)/shard_map/psum | solution.py:56
  374.7 8.3 collective-permute-start.2
  386.4 235.4 %all-reduce.27.cloned.1.call-start = ((), (), s32[]{:S(2)}) async-start(), calls=%async_computation.7 | async-start | bytes 1048576 | tf_op jit(solution)/shard_map/psum | solution.py:56
  499.3 8.3 collective-permute-start.3
  511.1 235.5 %all-reduce.29.cloned.1.call-start = ((), (), s32[]{:S(2)}) async-start(), calls=%async_computation.8 | async-start | bytes 1048576 | tf_op jit(solution)/shard_map/psum | solution.py:56
  623.9 8.3 collective-permute-start.4
  635.7 235.5 %all-reduce.31.cloned.1.call-start = ((), (), s32[]{:S(2)}) async-start(), calls=%async_computation.9 | async-start | bytes 1048576 | tf_op jit(solution)/shard_map/psum | solution.py:56
  748.6 8.3 collective-permute-start.5
  760.3 165.0 %all-reduce.33.cloned.1.call-start = ((), (), s32[]{:S(2)}) async-start(), calls=%async_computation.10 | async-start | bytes 2097152 | tf_op jit(solution)/shard_map/psum | solution.py:15
  871.1 3.2 copy-start.46
  871.1 3.5 copy-start.56
  873.1 53.7 %copy-start.40 = (bf16[1024,160]{0,1:T(8,128)(2,1)S(1)}, bf16[1024,160]{0,1:T(8,128)(2,1)}, u32[]{:S(2)}) copy-start(bf16[1024,160]{0,1:T(8,128)(2,1)} %param.11) | copy-start | bytes 983044
  874.2 180.6 %copy-start.55 = (s32[4,512]{1,0:T(4,128)S(1)}, s32[4,512]{1,0:T(4,128)}, u32[]{:S(2)}) copy-start(s32[4,512]{1,0:T(4,128)} %param.8) | copy-start | bytes 24580
  874.2 562.6 %all-gather.2.cloned.1.call-start = ((), (), s32[]{:S(2)}) async-start(), calls=%async_computation.11 | async-start | bytes 1064960 | tf_op jit(solution)/shard_map/all_gather | solution.py:125
  1361.0 190.8 %all-reduce.35.cloned.1.call-start = ((), (), s32[]{:S(2)}) async-start(), calls=%async_computation.12 | async-start | bytes 1048576 | tf_op jit(solution)/shard_map/psum | solution.py:56
  1361.4 192.6 %copy-start.51 = (f32[128]{0:T(128)}, f32[128]{0:T(128)S(1)}, u32[]{:S(2)}) copy-start(f32[128]{0:T(128)S(1)} %add_rsqrt_fusion.7) | copy-start | bytes 1540
  1361.8 80.3 %copy-start.29 = (f32[128,512]{1,0:T(8,128)}, f32[128,512]{1,0:T(8,128)S(1)}, u32[]{:S(2)}) copy-start(f32[128,512]{1,0:T(8,128)S(1)} %fusion.61) | copy-start | bytes 786436
  1439.3 2.2 copy-start.6
  1444.9 230.8 %all-reduce.37.cloned.1.call-start = ((), (), s32[]{:S(2)}) async-start(), calls=%async_computation.13 | async-start | bytes 1048576 | tf_op jit(solution)/shard_map/psum | solution.py:56
  1554.3 9.0 collective-permute-start.6
  1555.9 7.4 copy-start.19
  1565.8 235.3 %all-reduce.39.cloned.1.call-start = ((), (), s32[]{:S(2)}) async-start(), calls=%async_computation.14 | async-start | bytes 1048576 | tf_op jit(solution)/shard_map/psum | solution.py:56
  1678.3 9.0 collective-permute-start.7
  1680.6 8.9 copy-start.21
  1691.5 235.4 %all-reduce.41.cloned.1.call-start = ((), (), s32[]{:S(2)}) async-start(), calls=%async_computation.15 | async-start | bytes 1048576 | tf_op jit(solution)/shard_map/psum | solution.py:56
  1803.8 9.0 collective-permute-start.8
  1805.7 122.4 %copy-start.47 = (f32[128]{0:T(128)}, f32[128]{0:T(128)S(1)}, u32[]{:S(2)}) copy-start(f32[128]{0:T(128)S(1)} %add_rsqrt_fusion.4) | copy-start | bytes 1540
  1806.0 9.0 copy-start.23
  1817.0 235.6 %all-reduce.43.cloned.1.call-start = ((), (), s32[]{:S(2)}) async-start(), calls=%async_computation.16 | async-start | bytes 1048576 | tf_op jit(solution)/shard_map/psum | solution.py:56
  1929.5 9.0 collective-permute-start.9
  1931.4 122.5 %copy-start.49 = (f32[128]{0:T(128)}, f32[128]{0:T(128)S(1)}, u32[]{:S(2)}) copy-start(f32[128]{0:T(128)S(1)} %add_rsqrt_fusion.3) | copy-start | bytes 1540
  1931.7 9.0 copy-start.25
  1942.7 235.6 %all-reduce.45.cloned.1.call-start = ((), (), s32[]{:S(2)}) async-start(), calls=%async_computation.17 | async-start | bytes 1048576 | tf_op jit(solution)/shard_map/psum | solution.py:56
  2055.2 9.0 collective-permute-start.10
  2057.6 8.9 copy-start.27
  2068.5 149.3 %reduce-scatter.8.cloned.1.call-start = ((), (), s32[]{:S(2)}) async-start(), calls=%async_computation.20 | async-start | bytes 819200 | tf_op jit(solution)/shard_map/reduce_scatter | solution.py:157
  2071.2 170.0 %reduce-scatter.6.cloned.1.call-start = ((), (), s32[]{:S(2)}) async-start(), calls=%async_computation.19 | async-start | bytes 2621440 | tf_op jit(solution)/shard_map/reduce_scatter | solution.py:156
  2071.4 3.0 copy-start.20
  2071.5 4.8 copy-start.9
  2071.5 4.8 copy-start.22
  2074.4 3.6 copy-start.11
  2074.4 3.6 copy-start.24
  2076.2 3.6 copy-start.13
  2076.2 3.6 copy-start.26
  2078.0 3.7 copy-start.15
  2078.0 3.7 copy-start.28
  2178.3 12.4 copy-start.7
  2181.0 9.0 collective-permute-start.11
  2182.4 7.7 copy-start.53
  2197.5 78.8 %reduce-scatter.4.cloned.1.call-start = ((), (), s32[]{:S(2)}) async-start(), calls=%async_computation.18 | async-start | bytes 2621440 | tf_op jit(solution)/shard_map/reduce_scatter | solution.py:155
  2198.1 3.7 copy-start.33
  2200.0 3.7 copy-start.35
  2200.0 3.7 copy-start.48
  2201.8 3.8 copy-start.37
  2201.8 3.8 copy-start.50
  2203.7 3.8 copy-start.39
  2205.5 3.8 copy-start.54
  (23 other events, 22.3 us)
Sparse Core Ops, SparseCore 0:
  11.4 113.3 all-reduce.18
  137.1 110.8 all-reduce.20
  261.9 110.6 all-reduce.22
  386.6 110.6 all-reduce.24
  511.2 110.6 all-reduce.26
  635.8 110.6 all-reduce.28
  760.4 110.6 all-reduce.30
  874.4 50.9 all-reduce.32
  1361.2 75.6 all-gather.1
  1445.0 106.8 all-reduce.34
  1565.9 109.7 all-reduce.36
  1691.6 109.5 all-reduce.38
  1817.1 109.7 all-reduce.40
  1942.8 109.7 all-reduce.42
  2068.6 109.7 all-reduce.44
  2181.3 23.4 reduce-scatter.7
  2207.8 33.2 reduce-scatter.5
  2244.3 31.9 reduce-scatter.3
